TPU v7x, 256 devices: a whole 4x4x8 slice. The times are simulated.
256 devices in a mesh: band: 16 (over y, x), lev: 16 (over z, core).
Axes of the slice: x: 4, y: 4, z: 8, core: 2. Of those that a mesh axis runs over, the one named last changes fastest.
Arguments:
- adj_spec: bfloat16 [64, 1280, 2, 1280], P('lev', 'band'), may hold values from -6 to 6
- wave_of_slot: int32 [1280], replicated, may hold values from 0 to 1279, each once
- legendre: bfloat16 [1280, 32, 1280], P('band'), may hold values from -0.15625 to 0.15625
- lat_weight: float32 [32], replicated, may hold values from 0.5 to 1.5
- traj: bfloat16 [64, 64, 5136], P('lev', 'band'), may hold values from -3 to 3
- traj_exp: int32 [64, 64, 4], P('lev', 'band'), may hold values from -2 to 2
- traj_order: int32 [16, 4], P('lev'), may hold values from 0 to 3, each once within a row
- lev_coef: float32 [64], P('lev'), may hold values from 0.02 to 0.2
Outputs:
- adj_out: bfloat16 [64, 1280, 2, 1280], P('lev', 'band')
Inputs may be any that keep to these rules, and one draw needn't show every extreme that they name: `wave_of_slot`: every wavenumber 0 to 1279 is held by exactly one slot. `traj_order`: each row is a permutation of 0 to 3.
All inputs are finite; a program needn't handle non-finite values.
Results may differ from a plain program's by a relative error of at most 0.0085.
Values may be sent and summed in bfloat16 or wider, within the bound.
No kernel may reach another device: no remote copies, remote signals or barrier semaphores. Data moves between devices by JAX's collectives and lax.ppermute only.
A program may use at most 128 MiB of HBM per device.

v0:
```python
import math
import jax
import jax.numpy as jnp
from jax import lax
from jax.sharding import PartitionSpec as P

NBLK = 4
LO = 32


def angles(wave_ids, lon_ids, lon_count):
    phase = lon_ids[:, None] * wave_ids[None, :] % lon_count
    angle = phase.astype(jnp.float32) * (2.0 * math.pi / lon_count)
    return (jnp.cos(angle), jnp.sin(angle))


def quarter_table(wave_ids, width, lon_count):
    steps = -(-width // LO)
    low = angles(wave_ids, jnp.arange(LO, dtype=jnp.int32), lon_count)
    high = angles(wave_ids, jnp.arange(steps, dtype=jnp.int32) * LO, lon_count)
    cos_low, sin_low, cos_high, sin_high = lax.optimization_barrier((*low, *high))
    cos_high, sin_high = (cos_high[:, None], sin_high[:, None])
    cos_all = cos_high * cos_low - sin_high * sin_low
    sin_all = sin_high * cos_low + cos_high * sin_low
    flat = (steps * LO, wave_ids.shape[0])
    cos_all = cos_all.astype(jnp.bfloat16).reshape(flat)
    sin_all = (-sin_all).astype(jnp.bfloat16).reshape(flat)
    return lax.optimization_barrier((cos_all[:width], sin_all[:width]))


def scan_levels(total):
    size, axis = (16, "lev")
    running = total
    step = 1
    while step < size:
        moved = lax.ppermute(
            running.astype(jnp.bfloat16), axis, [(i, i + step) for i in range(size - step)]
        )
        running = running + moved.astype(jnp.float32)
        step *= 2
    return lax.ppermute(
        running.astype(jnp.bfloat16), axis, [(i, i + 1) for i in range(size - 1)]
    ).astype(jnp.float32)


def body(adj_spec, wave_of_slot, legendre, lat_weight, traj, traj_exp, traj_order, lev_coef):
    bf16, f32 = (jnp.bfloat16, jnp.float32)
    highest = lax.Precision.HIGHEST
    levels, slots, _, degrees = adj_spec.shape
    lat_rows, lon_count = traj.shape[1:]
    width = lon_count // NBLK
    norm_scale = 1.0 / math.sqrt(degrees)
    waves_here = lax.dynamic_slice_in_dim(wave_of_slot, lax.axis_index("band") * slots, slots)
    degree_ids = jnp.arange(degrees, dtype=jnp.int32)
    valid = degree_ids[None, :] < (degrees - waves_here)[:, None]
    masked = jnp.where(valid[None, :, None, :], adj_spec, jnp.zeros_like(adj_spec))
    sign = jnp.where(degree_ids % 2 == 0, 1.0, -1.0).astype(bf16)
    stacked = jnp.stack([masked, masked * sign], axis=3)
    side = jnp.einsum("lscej,shj->lsche", stacked, legendre, preferred_element_type=f32)
    weight_q = jnp.repeat(lat_weight, 2)
    fourier = (side.reshape(levels, slots, 2, -1) * weight_q).astype(bf16)
    fourier = lax.all_to_all(fourier, "band", split_axis=3, concat_axis=1, tiled=True)
    total = jnp.sum(fourier.astype(f32), axis=0)
    carry = scan_levels(total)
    cos_t, sin_t = quarter_table(wave_of_slot, width, lon_count)
    turn = jnp.arange(NBLK, dtype=jnp.int32)[:, None] * wave_of_slot[None, :] % 4
    cos_b = jnp.where(turn == 0, 1.0, jnp.where(turn == 2, -1.0, 0.0))
    sin_b = jnp.where(turn == 1, 1.0, jnp.where(turn == 3, -1.0, 0.0))

    def to_grid(rows):
        first, second = (rows[:, None, :, 0], rows[:, None, :, 1])
        first, second = (jnp.moveaxis(first, 2, 3), jnp.moveaxis(second, 2, 3))
        cb, sb = (cos_b[None, :, None, :], sin_b[None, :, None, :])
        with_cos = (first * cb - second * sb).astype(bf16)
        with_sin = (first * sb + second * cb).astype(bf16)
        out = jnp.einsum("lbqs,ks->lbqk", with_cos, cos_t, preferred_element_type=f32)
        out = out + jnp.einsum("lbqs,ks->lbqk", with_sin, sin_t, preferred_element_type=f32)
        return out * norm_scale

    grid = to_grid(fourier.astype(f32))
    group = to_grid(carry[None])
    running = jnp.cumsum(grid, axis=0)
    above = jnp.concatenate([jnp.zeros_like(grid[:1]), running[:-1]], axis=0) + group
    order = jnp.arange(levels, dtype=jnp.int32)
    select = (traj_order[0][None, :] == order[:, None]).astype(f32)
    scaled = traj.astype(f32).reshape(levels, lat_rows, NBLK, width)
    scaled = scaled * jnp.exp2(traj_exp.astype(f32))[..., None]
    ordered = jnp.einsum("ir,rqbk->ibqk", select, scaled, precision=highest)
    forcing = (1.0 + jnp.tanh(ordered)) * (grid + lev_coef[:, None, None, None] * above)
    forcing = forcing.astype(bf16)
    by_cos = jnp.einsum("lbqk,ks->lbqs", forcing, cos_t, preferred_element_type=f32)
    by_sin = jnp.einsum("lbqk,ks->lbqs", forcing, sin_t, preferred_element_type=f32)
    cb, sb = (cos_b[None, :, None, :], sin_b[None, :, None, :])
    first = jnp.sum(by_cos * cb + by_sin * sb, axis=1) * norm_scale
    second = jnp.sum(by_sin * cb - by_cos * sb, axis=1) * norm_scale
    analysis = jnp.stack([first, second], axis=1)
    halves = analysis.reshape(levels, 2, lat_rows // 2, 2, -1)
    sym = halves[:, :, :, 0] + halves[:, :, :, 1]
    anti = halves[:, :, :, 0] - halves[:, :, :, 1]
    sides = jnp.stack([sym, anti], axis=2).astype(bf16)
    sides = lax.all_to_all(sides, "band", split_axis=4, concat_axis=3, tiled=True)
    both = jnp.einsum("lcehs,shj->lsecj", sides, legendre, preferred_element_type=f32)
    result = jnp.where(degree_ids % 2 == 0, both[:, :, 0], both[:, :, 1])
    return jnp.where(valid[None, :, None, :], result, 0.0).astype(bf16)


def solution(mesh):
    return jax.shard_map(
        body,
        mesh=mesh,
        in_specs=(
            P("lev", "band", None, None),
            P(),
            P("band", None, None),
            P(),
            P("lev", "band", None),
            P("lev", "band", None),
            P("lev", None),
            P("lev"),
        ),
        out_specs=P("lev", "band", None, None),
        check_vma=False,
    )
```

profile of v0, /device:TPU:97, one launch (start us, length us, event | category | flops | bytes accessed | tf_op | source)
XLA Modules:
  0.0 117.2 jit_solution(4242895154096673147)
XLA Ops:
  1.5 3.5 %fusion.46 = (bf16[4,80,2,1,1280]{4,0,3,2,1:T(4,128)(2,1)S(1)}, bf16[4,80,2,1,1280]{4,0,3,2,1:T(4,128)(2,1)S(1)}) fusion(bf16[4,80,2,1280]{3,2,1,0:T(2,128)(2,1)} %param.8, pred[80,1280]{1,0:T(8,128)(4,1)S(1)} %iota_compare_fusion, bf16[1280]{0:T(1024)(128)(2,1)S(1)} %select_convert_fusion), kind=kLoop, calls=%fused_computation.39 | loop fusion | flops 1638400 | bytes 5020160 | tf_op jit(solution)/shard_map/stack | solution.py:58
  5.1 6.2 %fusion.41 = f32[4,80,2,32,2]{3,0,4,2,1:T(4,128)S(1)} fusion(bf16[80,32,1280]{2,1,0:T(8,128)(2,1)} %param.10, bf16[4,80,2,1,1280]{4,0,3,2,1:T(4,128)(2,1)S(1)} %get-tuple-element.20, bf16[4,80,2,1,1280]{4,0,3,2,1:T(4,128)(2,1)S(1)} %get-tuple-element.19), kind=kOutput, calls=%fused_computation.38 | convolution fusion | flops 111411200 | bytes 9994240 | tf_op jit(solution)/shard_map/lscej,shj->lsche/dot_general | solution.py:59
  12.6 6.8 %all-to-all-start = ((bf16[4,80,2,64]{1,2,0,3:T(2,128)(2,1)}), bf16[4,80,2,64]{1,2,0,3:T(2,128)(2,1)S(1)}, u32[]{:S(2)}, u32[]{:S(2)}) async-start(bf16[4,80,2,64]{1,2,0,3:T(2,128)(2,1)} %copy.62), calls=%async_computation | async-start | bytes 262144 | tf_op jit(solution)/shard_map/all_to_all | solution.py:62
  21.2 2.5 %negate_convert_fusion = (bf16[41,32,1280]{2,1,0:T(8,128)(2,1)S(1)}, bf16[41,32,1280]{2,1,0:T(8,128)(2,1)S(1)}) fusion(f32[32,1280]{1,0:T(8,128)S(1)} %get-tuple-element.14, f32[41,1280]{1,0:T(8,128)S(1)} %get-tuple-element.13, f32[32,1280]{1,0:T(8,128)S(1)} %get-tuple-element.12, f32[41,1280]{1,0:T(8,128)S(1)} %get-tuple-element.11), kind=kLoop, calls=%fused_computation | loop fusion | flops 15114240 | bytes 7464960 | tf_op jit(solution)/shard_map/convert_element_type | solution.py:27
  23.8 1.9 %slice.48 = bf16[1284,1280]{1,0:T(8,128)(2,1)} slice(bf16[1312,1280]{1,0:T(8,128)(2,1)S(1)} %bitcast.135), slice={[0:1284], [0:1280]} | slice | bytes 6574080 | tf_op jit(solution)/shard_map/slice | solution.py:28
  25.9 1.9 %reshape.192 = f32[4,4,4,1284]{3,2,1,0:T(4,128)} reshape(bf16[4,4,5136]{2,1,0:T(4,128)(2,1)} %param.12) | data formatting | bytes 493056 | tf_op jit(solution)/shard_map/reshape | solution.py:86
  30.1 5.6 %collective-permute-start = (bf16[1280,2,4]{0,2,1:T(4,128)(2,1)S(1)}, bf16[1280,2,4]{0,2,1:T(4,128)(2,1)S(1)}, u32[]{:S(2)}, u32[]{:S(2)}) collective-permute-start(bf16[1280,2,4]{0,2,1:T(4,128)(2,1)S(1)} %convert_element_type.122), channel_id=1, source_target_pairs={{0,1},{1,2},{2,3},{3,4},{4,5},{5,6},{6,7},{7,8},{8,9},{9,10},{10,1... | collective-permute-start | bytes 61448 | tf_op jit(solution)/shard_map/ppermute | solution.py:36
  36.5 1.8 %reshape.193 = f32[4,1280,2,4]{1,3,2,0:T(4,128)} reshape(f32[4,16,80,2,4]{2,1,4,3,0:T(8,128)} %copy.64) | data formatting | bytes 327680 | tf_op jit(solution)/shard_map/convert_element_type | solution.py:80
  38.3 2.6 %collective-permute-start.1 = (bf16[1280,2,4]{0,2,1:T(4,128)(2,1)S(1)}, bf16[1280,2,4]{0,2,1:T(4,128)(2,1)S(1)}, u32[]{:S(2)}, u32[]{:S(2)}) collective-permute-start(bf16[1280,2,4]{0,2,1:T(4,128)(2,1)S(1)} %fusion.78), channel_id=1, source_target_pairs={{0,2},{1,3},{2,4},{3,5},{4,6},{5,7},{6,8},{7,9},{8,10},{9,11},{10,... | collective-permute-start | bytes 61448 | tf_op jit(solution)/shard_map/ppermute | solution.py:36
  42.9 3.1 %collective-permute-start.2 = (bf16[1280,2,4]{0,2,1:T(4,128)(2,1)S(1)}, bf16[1280,2,4]{0,2,1:T(4,128)(2,1)S(1)}, u32[]{:S(2)}, u32[]{:S(2)}) collective-permute-start(bf16[1280,2,4]{0,2,1:T(4,128)(2,1)S(1)} %fusion.89), channel_id=1, source_target_pairs={{0,4},{1,5},{2,6},{3,7},{4,8},{5,9},{6,10},{7,11},{8,12},{9,13},{1... | collective-permute-start | bytes 61448 | tf_op jit(solution)/shard_map/ppermute | solution.py:36
  46.2 2.1 %collective-permute-done.2 = bf16[1280,2,4]{0,2,1:T(4,128)(2,1)S(1)} collective-permute-done((bf16[1280,2,4]{0,2,1:T(4,128)(2,1)S(1)}, bf16[1280,2,4]{0,2,1:T(4,128)(2,1)S(1)}, u32[]{:S(2)}, u32[]{:S(2)}) %collective-permute-start.2) | collective-permute-done | bytes 20512 | tf_op jit(solution)/shard_map/ppermute | solution.py:36
  48.3 3.3 %collective-permute-start.3 = (bf16[1280,2,4]{0,2,1:T(4,128)(2,1)S(1)}, bf16[1280,2,4]{0,2,1:T(4,128)(2,1)S(1)}, u32[]{:S(2)}, u32[]{:S(2)}) collective-permute-start(bf16[1280,2,4]{0,2,1:T(4,128)(2,1)S(1)} %fusion.79), channel_id=1, source_target_pairs={{0,8},{1,9},{2,10},{3,11},{4,12},{5,13},{6,14},{7,15},{16,24},{17,... | collective-permute-start | bytes 61448 | tf_op jit(solution)/shard_map/ppermute | solution.py:36
  52.9 13.7 %collective-permute-start.4 = (bf16[1280,2,4]{0,2,1:T(4,128)(2,1)S(1)}, bf16[1280,2,4]{0,2,1:T(4,128)(2,1)S(1)}, u32[]{:S(2)}, u32[]{:S(2)}) collective-permute-start(bf16[1280,2,4]{0,2,1:T(4,128)(2,1)S(1)} %add_convert_fusion.4), channel_id=1, source_target_pairs={{0,1},{1,2},{2,3},{3,4},{4,5},{5,6},{6,7},{7,8},{8,9},{9,10},{10,1... | collective-permute-start | bytes 61448 | tf_op jit(solution)/shard_map/ppermute | solution.py:41
  66.6 2.0 %fusion.28 = f32[4,4,4,1284]{3,0,1,2:T(4,128)} fusion(f32[4,4,4,1284]{3,0,1,2:T(4,128)S(1)} %fusion.15, bf16[1284,1280]{1,0:T(8,128)(2,1)S(1)} %copy-done, bf16[4,4,4,1280]{3,2,1,0:T(4,128)(2,1)S(1)} %get-tuple-element.23), kind=kOutput, calls=%fused_computation.28 | convolution fusion | flops 210534912 | bytes 4108288 | tf_op jit(solution)/shard_map/lbqs,ks->lbqk/dot_general | solution.py:76
  68.6 2.2 %reduce_window_sum.11 = f32[4,4,4,1284]{3,0,1,2:T(4,128)} reduce-window(f32[4,4,4,1284]{3,0,1,2:T(4,128)} %fusion.28, f32[]{:T(128)} %constant.88.clone.1), window={size=4x1x1x1 pad=3_0x0_0x0_0x0_0}, to_apply=%region_0.1 | reduce-window | flops 246528 | bytes 657412 | tf_op jit(solution)/shard_map/jit(cumsum)/reduce_window_sum | solution.py:82
  76.6 3.5 %copy.75 = bf16[4,2,2,2,1280]{0,3,1,2,4:T(2,128)(2,1)S(1)} copy(bf16[4,2,2,2,1280]{4,0,3,1,2:T(4,128)(2,1)S(1)} %pad_maximum_fusion.1) | data formatting | bytes 163840 | tf_op jit(solution)/shard_map/stack | solution.py:100
  80.2 5.7 %reshape.202 = bf16[16,2,1280]{2,1,0:T(2,128)(2,1)} reshape(bf16[1280,2,2,2,4]{4,3,2,1,0:T(2,128)(2,1)S(1)} %bitcast.136) | data formatting | bytes 163840
  85.9 6.9 %all-to-all-start.1 = ((bf16[16,2,1280]{2,1,0:T(2,128)(2,1)}), bf16[16,2,1280]{2,1,0:T(2,128)(2,1)S(1)}, u32[]{:S(2)}, u32[]{:S(2)}) async-start(bf16[16,2,1280]{2,1,0:T(2,128)(2,1)} %reshape.202), calls=%async_computation.1 | async-start | bytes 163840 | tf_op jit(solution)/shard_map/all_to_all | solution.py:101
  92.8 6.6 %all-to-all-done.1 = bf16[16,2,1280]{2,1,0:T(2,128)(2,1)S(1)} async-done(((bf16[16,2,1280]{2,1,0:T(2,128)(2,1)}), bf16[16,2,1280]{2,1,0:T(2,128)(2,1)S(1)}, u32[]{:S(2)}, u32[]{:S(2)}) %all-to-all-start.1) | async-done | bytes 81952 | tf_op jit(solution)/shard_map/all_to_all | solution.py:101
  99.4 5.6 %reshape.203 = bf16[1280,2,2,2,4]{4,3,2,1,0:T(2,128)(2,1)S(1)} reshape(bf16[16,2,1280]{2,1,0:T(2,128)(2,1)S(1)} %all-to-all-done.1) | data formatting | bytes 163840
  105.0 3.6 %copy.93 = bf16[4,2,2,2,16,80]{5,4,3,2,1,0:T(8,128)(2,1)S(1)} copy(bf16[4,2,2,2,16,80]{0,3,1,2,5,4:T(2,128)(2,1)S(1)} %bitcast.137) | data formatting | bytes 163840 | tf_op jit(solution)/shard_map/all_to_all | solution.py:101
  109.0 4.2 %fusion.4 = bf16[4,80,2,2,1280]{4,0,3,1,2:T(4,128)(2,1)S(1)} fusion(bf16[4,2,2,32,80]{3,0,1,4,2:T(4,128)(2,1)S(1)} %copy.89, bf16[80,32,1280]{2,1,0:T(8,128)(2,1)} %param.10), kind=kOutput, calls=%fused_computation.6 | convolution fusion | flops 104857600 | bytes 9912320 | tf_op jit(solution)/shard_map/lcehs,shj->lsecj/dot_general | solution.py:102
  113.2 1.6 %fusion.21 = bf16[4,80,2,1280]{3,0,2,1:T(4,128)(2,1)S(1)} fusion(bf16[4,80,2,2,1280]{4,0,3,1,2:T(4,128)(2,1)S(1)} %fusion.4, pred[1280]{0:T(1024)(128)(4,1)S(1)} %fusion.81, pred[80,1280]{1,0:T(8,128)(4,1)S(1)} %copy-done.3), kind=kLoop, calls=%fused_computation.22 | loop fusion | flops 1638400 | bytes 5018880 | tf_op jit(solution)/shard_map/convert_element_type | solution.py:104
  114.8 2.4 %copy.80 = bf16[4,80,2,1280]{3,2,1,0:T(2,128)(2,1)} copy(bf16[4,80,2,1280]{3,0,2,1:T(4,128)(2,1)S(1)} %fusion.21) | data formatting | bytes 3276800 | tf_op jit(solution)/shard_map/convert_element_type | solution.py:104
  (75 shorter events, 17.4 us)
Async XLA Ops:
  0.9 0.6 copy-start.2
  5.1 6.5 %copy-start.10 = (f32[32]{0:T(128)S(1)}, f32[32]{0:T(128)}, u32[]{:S(2)}) copy-start(f32[32]{0:T(128)} %param.11) | copy-start | bytes 388
  5.1 14.3 %copy-start.7 = (s32[1280]{0:T(1024)S(1)}, s32[1280]{0:T(1024)}, u32[]{:S(2)}) copy-start(s32[1280]{0:T(1024)} %param.9) | copy-start | bytes 15364
  12.6 15.9 %all-to-all-start = ((bf16[4,80,2,64]{1,2,0,3:T(2,128)(2,1)}), bf16[4,80,2,64]{1,2,0,3:T(2,128)(2,1)S(1)}, u32[]{:S(2)}, u32[]{:S(2)}) async-start(bf16[4,80,2,64]{1,2,0,3:T(2,128)(2,1)} %copy.62), calls=%async_computation | async-start | bytes 262144 | tf_op jit(solution)/shard_map/all_to_all | solution.py:62
  21.2 2.5 %copy-start.8 = (s32[4,4,4]{2,1,0:T(4,128)S(1)}, s32[4,4,4]{2,1,0:T(4,128)}, u32[]{:S(2)}) copy-start(s32[4,4,4]{2,1,0:T(4,128)} %param.13) | copy-start | bytes 772
  30.1 8.2 %collective-permute-start = (bf16[1280,2,4]{0,2,1:T(4,128)(2,1)S(1)}, bf16[1280,2,4]{0,2,1:T(4,128)(2,1)S(1)}, u32[]{:S(2)}, u32[]{:S(2)}) collective-permute-start(bf16[1280,2,4]{0,2,1:T(4,128)(2,1)S(1)} %convert_element_type.122), channel_id=1, source_target_pairs={{0,1},{1,2},{2,3},{3,4},{4,5},{5,6},{6,7},{7,8},{8,9},{9,10},{10,1... | collective-permute-start | bytes 61448 | tf_op jit(solution)/shard_map/ppermute | solution.py:36
  38.3 4.5 %collective-permute-start.1 = (bf16[1280,2,4]{0,2,1:T(4,128)(2,1)S(1)}, bf16[1280,2,4]{0,2,1:T(4,128)(2,1)S(1)}, u32[]{:S(2)}, u32[]{:S(2)}) collective-permute-start(bf16[1280,2,4]{0,2,1:T(4,128)(2,1)S(1)} %fusion.78), channel_id=1, source_target_pairs={{0,2},{1,3},{2,4},{3,5},{4,6},{5,7},{6,8},{7,9},{8,10},{9,11},{10,... | collective-permute-start | bytes 61448 | tf_op jit(solution)/shard_map/ppermute | solution.py:36
  42.9 5.4 %collective-permute-start.2 = (bf16[1280,2,4]{0,2,1:T(4,128)(2,1)S(1)}, bf16[1280,2,4]{0,2,1:T(4,128)(2,1)S(1)}, u32[]{:S(2)}, u32[]{:S(2)}) collective-permute-start(bf16[1280,2,4]{0,2,1:T(4,128)(2,1)S(1)} %fusion.89), channel_id=1, source_target_pairs={{0,4},{1,5},{2,6},{3,7},{4,8},{5,9},{6,10},{7,11},{8,12},{9,13},{1... | collective-permute-start | bytes 61448 | tf_op jit(solution)/shard_map/ppermute | solution.py:36
  46.2 20.4 %copy-start = (bf16[1284,1280]{1,0:T(8,128)(2,1)S(1)}, bf16[1284,1280]{1,0:T(8,128)(2,1)}, u32[]{:S(2)}) copy-start(bf16[1284,1280]{1,0:T(8,128)(2,1)} %slice.48) | copy-start | bytes 9861124
  48.3 4.5 %collective-permute-start.3 = (bf16[1280,2,4]{0,2,1:T(4,128)(2,1)S(1)}, bf16[1280,2,4]{0,2,1:T(4,128)(2,1)S(1)}, u32[]{:S(2)}, u32[]{:S(2)}) collective-permute-start(bf16[1280,2,4]{0,2,1:T(4,128)(2,1)S(1)} %fusion.79), channel_id=1, source_target_pairs={{0,8},{1,9},{2,10},{3,11},{4,12},{5,13},{6,14},{7,15},{16,24},{17,... | collective-permute-start | bytes 61448 | tf_op jit(solution)/shard_map/ppermute | solution.py:36
  52.9 17.9 %collective-permute-start.4 = (bf16[1280,2,4]{0,2,1:T(4,128)(2,1)S(1)}, bf16[1280,2,4]{0,2,1:T(4,128)(2,1)S(1)}, u32[]{:S(2)}, u32[]{:S(2)}) collective-permute-start(bf16[1280,2,4]{0,2,1:T(4,128)(2,1)S(1)} %add_convert_fusion.4), channel_id=1, source_target_pairs={{0,1},{1,2},{2,3},{3,4},{4,5},{5,6},{6,7},{7,8},{8,9},{9,10},{10,1... | collective-permute-start | bytes 61448 | tf_op jit(solution)/shard_map/ppermute | solution.py:41
  70.8 1.9 %copy-start.1 = (bf16[1284,1280]{1,0:T(8,128)(2,1)S(1)}, bf16[1284,1280]{1,0:T(8,128)(2,1)}, u32[]{:S(2)}) copy-start(bf16[1284,1280]{1,0:T(8,128)(2,1)} %slice.48) | copy-start | bytes 9861124
  70.8 3.0 %copy-start.4 = (f32[4,4,4,1284]{3,2,1,0:T(4,128)S(1)}, f32[4,4,4,1284]{3,2,1,0:T(4,128)}, u32[]{:S(2)}) copy-start(f32[4,4,4,1284]{3,2,1,0:T(4,128)} %reshape.192) | copy-start | bytes 986116
  70.8 3.0 %copy-start.5 = (f32[4,4,4,1284]{3,0,1,2:T(4,128)S(1)}, f32[4,4,4,1284]{3,0,1,2:T(4,128)}, u32[]{:S(2)}) copy-start(f32[4,4,4,1284]{3,0,1,2:T(4,128)} %fusion.28) | copy-start | bytes 986116
  70.8 3.0 %copy-start.6 = (f32[4,4,4,1284]{3,0,1,2:T(4,128)S(1)}, f32[4,4,4,1284]{3,0,1,2:T(4,128)}, u32[]{:S(2)}) copy-start(f32[4,4,4,1284]{3,0,1,2:T(4,128)} %reduce_window_sum.11) | copy-start | bytes 986116
  70.9 3.0 %copy-start.9 = (f32[4,4,4]{0,2,1:T(4,128)S(1)}, f32[4,4,4]{0,2,1:T(4,128)}, u32[]{:S(2)}) copy-start(f32[4,4,4]{0,2,1:T(4,128)} %copy.57) | copy-start | bytes 772
  70.9 3.0 %copy-start.11 = (f32[4]{0:T(128)S(1)}, f32[4]{0:T(128)}, u32[]{:S(2)}) copy-start(f32[4]{0:T(128)} %param.15) | copy-start | bytes 52
  70.9 3.0 %copy-start.12 = (s32[1,4]{1,0:T(1,128)S(1)}, s32[1,4]{1,0:T(1,128)}, u32[]{:S(2)}) copy-start(s32[1,4]{1,0:T(1,128)} %param.14) | copy-start | bytes 52
  85.9 13.5 %all-to-all-start.1 = ((bf16[16,2,1280]{2,1,0:T(2,128)(2,1)}), bf16[16,2,1280]{2,1,0:T(2,128)(2,1)S(1)}, u32[]{:S(2)}, u32[]{:S(2)}) async-start(bf16[16,2,1280]{2,1,0:T(2,128)(2,1)} %reshape.202), calls=%async_computation.1 | async-start | bytes 163840 | tf_op jit(solution)/shard_map/all_to_all | solution.py:101
  109.0 4.2 %copy-start.3 = (pred[80,1280]{1,0:T(8,128)(4,1)S(1)}, pred[80,1280]{1,0:T(8,128)(4,1)}, u32[]{:S(2)}) copy-start(pred[80,1280]{1,0:T(8,128)(4,1)} %copy-done.2) | copy-start | bytes 307204
where the time goes:
time: 118 us; the launch traced here: 117 us
  starting transfers between devices  42 us (36%)
  local copies, waits for them, and re-layouts  33.8 us (29%)
  matrix products  18.2 us (15%)
  other arithmetic  13.1 us (11%)
  waiting for transfers between devices  9.62 us (8%)
    ppermute x4, starting transfers between devices, scan_levels(): lax.ppermute(running.astype(jnp.bfloat16), axis, [(i, i + step) for i in...  14.6 us
    ppermute x1, starting transfers between devices, scan_levels(): lax.ppermute(running.astype(jnp.bfloat16), axis, [(i, i + 1) for i in ran...  13.7 us
    unnamed x28, local copies, waits for them, and re-layouts  12.8 us
    all_to_all x1, starting transfers between devices, body(): lax.all_to_all(sides, 'band', split_axis=4, concat_axis=3, tiled=True)  6.95 us
    all_to_all x1, starting transfers between devices, body(): lax.all_to_all(fourier, 'band', split_axis=3, concat_axis=1, tiled=True)  6.75 us
    all_to_all x1, waiting for transfers between devices, body(): lax.all_to_all(sides, 'band', split_axis=4, concat_axis=3, tiled=True)  6.56 us
    dot_general x1, matrix products, body(): jnp.einsum('lscej,shj->lsche', stacked, legendre, preferred_element_type=...  6.16 us
    dot_general x1, matrix products, body(): jnp.einsum('lcehs,shj->lsecj', sides, legendre, preferred_element_type=f32)  4.15 us
  transfers between devices with their start and end apart: 7, of which 3 were waited for; matrix products, arithmetic and copies ran while one was open for 15% of the time, Pallas kernels for 0%

commit v1 on v0

--- a/solution.py
+++ b/solution.py
@@ -98,7 +98,10 @@
     sym = halves[:, :, :, 0] + halves[:, :, :, 1]
     anti = halves[:, :, :, 0] - halves[:, :, :, 1]
     sides = jnp.stack([sym, anti], axis=2).astype(bf16)
-    sides = lax.all_to_all(sides, "band", split_axis=4, concat_axis=3, tiled=True)
+    sides = jnp.concatenate(
+        lax.all_to_all(jnp.stack(jnp.split(sides, lax.axis_size("band"), axis=4)), "band", 0, 0),
+        axis=3,
+    )
     both = jnp.einsum("lcehs,shj->lsecj", sides, legendre, preferred_element_type=f32)
     result = jnp.where(degree_ids % 2 == 0, both[:, :, 0], both[:, :, 1])
     return jnp.where(valid[None, :, None, :], result, 0.0).astype(bf16)

time: 118 us -> 110 us (0.932)
  local copies, waits for them, and re-layouts: 33.8 us -> 15.4 us
  other arithmetic: 13.1 us -> 23.7 us
    unnamed x28 -> x26, local copies, waits for them, and re-layouts: 12.8 us -> 1.48 us
    unnamed x0 -> x15, other arithmetic: none -> 9.99 us
    all_to_all x3 -> x0, local copies, waits for them, and re-layouts: 3.95 us -> none  [body(): lax.all_to_all(sides, 'band', split_axis=4, concat_axis=3, tiled=True)]
    another operation x1 -> x0, local copies, waits for them, and re-layouts: 3.52 us -> none  [body(): sides = jnp.stack([sym, anti], axis=2).astype(bf16)]
  transfers between devices with their start and end apart: 7 -> 7, of which waited for: 3 -> 3; matrix products, arithmetic and copies ran while one was open for 15% -> 17% of each run, Pallas kernels for 0% -> 0%
where the time goes in v1:
time: 110 us
  starting transfers between devices  42 us (38%)
  other arithmetic  23.7 us (22%)
  matrix products  18.2 us (17%)
  local copies, waits for them, and re-layouts  15.4 us (14%)
  waiting for transfers between devices  9.89 us (9%)
    ppermute x4, starting transfers between devices, scan_levels(): lax.ppermute(running.astype(jnp.bfloat16), axis, [(i, i + step) for i in...  14.6 us
    ppermute x1, starting transfers between devices, scan_levels(): lax.ppermute(running.astype(jnp.bfloat16), axis, [(i, i + 1) for i in ran...  13.7 us
    unnamed x15, other arithmetic  9.99 us
    all_to_all x1, starting transfers between devices, body(): lax.all_to_all(jnp.stack(jnp.split(sides, lax.axis_size('band'), axis=4))...  6.93 us
    all_to_all x1, waiting for transfers between devices, body(): lax.all_to_all(jnp.stack(jnp.split(sides, lax.axis_size('band'), axis=4))...  6.83 us
    all_to_all x1, starting transfers between devices, body(): lax.all_to_all(fourier, 'band', split_axis=3, concat_axis=1, tiled=True)  6.75 us
    dot_general x1, matrix products, body(): jnp.einsum('lscej,shj->lsche', stacked, legendre, preferred_element_type=...  6.16 us
    dot_general x1, matrix products, body(): jnp.einsum('lcehs,shj->lsecj', sides, legendre, preferred_element_type=f32)  4.15 us
  transfers between devices with their start and end apart: 7, of which 3 were waited for; matrix products, arithmetic and copies ran while one was open for 17% of the time, Pallas kernels for 0%

profile of v1, /device:TPU:97, one launch (start us, length us, event | category | flops | bytes accessed | tf_op | source)
XLA Modules:
  0.0 109.6 jit_solution(15615530718381744761)
XLA Ops:
  1.5 3.5 %fusion.46 = (bf16[4,80,2,1,1280]{4,0,3,2,1:T(4,128)(2,1)S(1)}, bf16[4,80,2,1,1280]{4,0,3,2,1:T(4,128)(2,1)S(1)}) fusion(bf16[4,80,2,1280]{3,2,1,0:T(2,128)(2,1)} %param.8, pred[80,1280]{1,0:T(8,128)(4,1)S(1)} %iota_compare_fusion, bf16[1280]{0:T(1024)(128)(2,1)S(1)} %select_convert_fusion), kind=kLoop, calls=%fused_computation.39 | loop fusion | flops 1638400 | bytes 5020160 | tf_op jit(solution)/shard_map/stack | solution.py:58
  5.1 6.2 %fusion.41 = f32[4,80,2,32,2]{3,0,4,2,1:T(4,128)S(1)} fusion(bf16[80,32,1280]{2,1,0:T(8,128)(2,1)} %param.10, bf16[4,80,2,1,1280]{4,0,3,2,1:T(4,128)(2,1)S(1)} %get-tuple-element.20, bf16[4,80,2,1,1280]{4,0,3,2,1:T(4,128)(2,1)S(1)} %get-tuple-element.19), kind=kOutput, calls=%fused_computation.38 | convolution fusion | flops 111411200 | bytes 9994240 | tf_op jit(solution)/shard_map/lscej,shj->lsche/dot_general | solution.py:59
  12.6 6.8 %all-to-all-start = ((bf16[4,80,2,64]{1,2,0,3:T(2,128)(2,1)}), bf16[4,80,2,64]{1,2,0,3:T(2,128)(2,1)S(1)}, u32[]{:S(2)}, u32[]{:S(2)}) async-start(bf16[4,80,2,64]{1,2,0,3:T(2,128)(2,1)} %copy.81), calls=%async_computation | async-start | bytes 262144 | tf_op jit(solution)/shard_map/all_to_all | solution.py:62
  20.1 1.1 fusion.51
  21.2 2.5 %negate_convert_fusion = (bf16[41,32,1280]{2,1,0:T(8,128)(2,1)S(1)}, bf16[41,32,1280]{2,1,0:T(8,128)(2,1)S(1)}) fusion(f32[32,1280]{1,0:T(8,128)S(1)} %get-tuple-element.14, f32[41,1280]{1,0:T(8,128)S(1)} %get-tuple-element.13, f32[32,1280]{1,0:T(8,128)S(1)} %get-tuple-element.12, f32[41,1280]{1,0:T(8,128)S(1)} %get-tuple-element.11), kind=kLoop, calls=%fused_computation | loop fusion | flops 15114240 | bytes 7464960 | tf_op jit(solution)/shard_map/convert_element_type | solution.py:27
  23.8 1.9 %slice.48 = bf16[1284,1280]{1,0:T(8,128)(2,1)} slice(bf16[1312,1280]{1,0:T(8,128)(2,1)S(1)} %bitcast.178), slice={[0:1284], [0:1280]} | slice | bytes 6574080 | tf_op jit(solution)/shard_map/slice | solution.py:28
  25.9 1.9 %reshape.200 = f32[4,4,4,1284]{3,2,1,0:T(4,128)} reshape(bf16[4,4,5136]{2,1,0:T(4,128)(2,1)} %param.12) | data formatting | bytes 493056 | tf_op jit(solution)/shard_map/reshape | solution.py:86
  30.2 5.6 %collective-permute-start = (bf16[1280,2,4]{0,2,1:T(4,128)(2,1)S(1)}, bf16[1280,2,4]{0,2,1:T(4,128)(2,1)S(1)}, u32[]{:S(2)}, u32[]{:S(2)}) collective-permute-start(bf16[1280,2,4]{0,2,1:T(4,128)(2,1)S(1)} %convert_element_type.122), channel_id=1, source_target_pairs={{0,1},{1,2},{2,3},{3,4},{4,5},{5,6},{6,7},{7,8},{8,9},{9,10},{10,1... | collective-permute-start | bytes 61448 | tf_op jit(solution)/shard_map/ppermute | solution.py:36
  36.5 1.8 %reshape.201 = f32[4,1280,2,4]{1,3,2,0:T(4,128)} reshape(f32[4,16,80,2,4]{2,1,4,3,0:T(8,128)} %copy.83) | data formatting | bytes 327680 | tf_op jit(solution)/shard_map/convert_element_type | solution.py:80
  38.3 2.6 %collective-permute-start.1 = (bf16[1280,2,4]{0,2,1:T(4,128)(2,1)S(1)}, bf16[1280,2,4]{0,2,1:T(4,128)(2,1)S(1)}, u32[]{:S(2)}, u32[]{:S(2)}) collective-permute-start(bf16[1280,2,4]{0,2,1:T(4,128)(2,1)S(1)} %fusion.79), channel_id=1, source_target_pairs={{0,2},{1,3},{2,4},{3,5},{4,6},{5,7},{6,8},{7,9},{8,10},{9,11},{10,... | collective-permute-start | bytes 61448 | tf_op jit(solution)/shard_map/ppermute | solution.py:36
  42.9 3.1 %collective-permute-start.2 = (bf16[1280,2,4]{0,2,1:T(4,128)(2,1)S(1)}, bf16[1280,2,4]{0,2,1:T(4,128)(2,1)S(1)}, u32[]{:S(2)}, u32[]{:S(2)}) collective-permute-start(bf16[1280,2,4]{0,2,1:T(4,128)(2,1)S(1)} %fusion.106), channel_id=1, source_target_pairs={{0,4},{1,5},{2,6},{3,7},{4,8},{5,9},{6,10},{7,11},{8,12},{9,13},{1... | collective-permute-start | bytes 61448 | tf_op jit(solution)/shard_map/ppermute | solution.py:36
  46.2 2.1 %collective-permute-done.2 = bf16[1280,2,4]{0,2,1:T(4,128)(2,1)S(1)} collective-permute-done((bf16[1280,2,4]{0,2,1:T(4,128)(2,1)S(1)}, bf16[1280,2,4]{0,2,1:T(4,128)(2,1)S(1)}, u32[]{:S(2)}, u32[]{:S(2)}) %collective-permute-start.2) | collective-permute-done | bytes 20512 | tf_op jit(solution)/shard_map/ppermute | solution.py:36
  48.4 3.3 %collective-permute-start.3 = (bf16[1280,2,4]{0,2,1:T(4,128)(2,1)S(1)}, bf16[1280,2,4]{0,2,1:T(4,128)(2,1)S(1)}, u32[]{:S(2)}, u32[]{:S(2)}) collective-permute-start(bf16[1280,2,4]{0,2,1:T(4,128)(2,1)S(1)} %fusion.80), channel_id=1, source_target_pairs={{0,8},{1,9},{2,10},{3,11},{4,12},{5,13},{6,14},{7,15},{16,24},{17,... | collective-permute-start | bytes 61448 | tf_op jit(solution)/shard_map/ppermute | solution.py:36
  51.6 1.2 %fusion.15 = f32[4,4,4,1284]{3,0,1,2:T(4,128)S(1)} fusion(bf16[1284,1280]{1,0:T(8,128)(2,1)S(1)} %slice.49, bf16[4,4,4,1280]{3,2,1,0:T(4,128)(2,1)S(1)} %get-tuple-element.24), kind=kOutput, calls=%fused_computation.15 | convolution fusion | flops 210370560 | bytes 3779584 | tf_op jit(solution)/shard_map/lbqs,ks->lbqk/dot_general | solution.py:77
  52.9 13.7 %collective-permute-start.4 = (bf16[1280,2,4]{0,2,1:T(4,128)(2,1)S(1)}, bf16[1280,2,4]{0,2,1:T(4,128)(2,1)S(1)}, u32[]{:S(2)}, u32[]{:S(2)}) collective-permute-start(bf16[1280,2,4]{0,2,1:T(4,128)(2,1)S(1)} %add_convert_fusion.3), channel_id=1, source_target_pairs={{0,1},{1,2},{2,3},{3,4},{4,5},{5,6},{6,7},{7,8},{8,9},{9,10},{10,1... | collective-permute-start | bytes 61448 | tf_op jit(solution)/shard_map/ppermute | solution.py:41
  66.6 2.0 %fusion.28 = f32[4,4,4,1284]{3,0,1,2:T(4,128)} fusion(f32[4,4,4,1284]{3,0,1,2:T(4,128)S(1)} %fusion.15, bf16[1284,1280]{1,0:T(8,128)(2,1)S(1)} %copy-done, bf16[4,4,4,1280]{3,2,1,0:T(4,128)(2,1)S(1)} %get-tuple-element.23), kind=kOutput, calls=%fused_computation.28 | convolution fusion | flops 210534912 | bytes 4108288 | tf_op jit(solution)/shard_map/lbqs,ks->lbqk/dot_general | solution.py:76
  68.7 2.2 %reduce_window_sum.11 = f32[4,4,4,1284]{3,0,1,2:T(4,128)} reduce-window(f32[4,4,4,1284]{3,0,1,2:T(4,128)} %fusion.28, f32[]{:T(128)} %constant.88.clone.1), window={size=4x1x1x1 pad=3_0x0_0x0_0x0_0}, to_apply=%region_0.1 | reduce-window | flops 246528 | bytes 657412 | tf_op jit(solution)/shard_map/jit(cumsum)/reduce_window_sum | solution.py:82
  70.9 1.0 fusion.11
  72.7 1.0 fusion.38
  87.3 6.9 %all-to-all-start.1 = ((bf16[16,4,2,2,2,80]{5,1,4,2,3,0:T(4,128)(2,1)}), bf16[16,4,2,2,2,80]{5,1,4,2,3,0:T(4,128)(2,1)S(1)}, u32[]{:S(2)}, u32[]{:S(2)}) async-start(bf16[16,4,2,2,2,80]{5,1,4,2,3,0:T(4,128)(2,1)} %constant_dynamic-update-slice_fusion), calls=%async_computation.1 | async-start | bytes 262144 | tf_op jit(solution)/shard_map/all_to_all | solution.py:102
  94.2 6.8 %all-to-all-done.1 = bf16[16,4,2,2,2,80]{5,1,4,2,3,0:T(4,128)(2,1)S(1)} async-done(((bf16[16,4,2,2,2,80]{5,1,4,2,3,0:T(4,128)(2,1)}), bf16[16,4,2,2,2,80]{5,1,4,2,3,0:T(4,128)(2,1)S(1)}, u32[]{:S(2)}, u32[]{:S(2)}) %all-to-all-start.1) | async-done | bytes 81952 | tf_op jit(solution)/shard_map/all_to_all | solution.py:102
  101.4 4.1 %fusion.4 = bf16[4,80,2,2,1280]{4,0,3,1,2:T(4,128)(2,1)S(1)} fusion(bf16[4,2,2,32,80]{3,0,1,4,2:T(4,128)(2,1)S(1)} %copy.109, bf16[80,32,1280]{2,1,0:T(8,128)(2,1)} %param.10), kind=kOutput, calls=%fused_computation.6 | convolution fusion | flops 104857600 | bytes 9912320 | tf_op jit(solution)/shard_map/lcehs,shj->lsecj/dot_general | solution.py:105
  105.6 1.6 %fusion.21 = bf16[4,80,2,1280]{3,0,2,1:T(4,128)(2,1)S(1)} fusion(bf16[4,80,2,2,1280]{4,0,3,1,2:T(4,128)(2,1)S(1)} %fusion.4, pred[1280]{0:T(1024)(128)(4,1)S(1)} %fusion.97, pred[80,1280]{1,0:T(8,128)(4,1)S(1)} %copy-done.3), kind=kLoop, calls=%fused_computation.22 | loop fusion | flops 1638400 | bytes 5018880 | tf_op jit(solution)/shard_map/convert_element_type | solution.py:107
  107.2 2.4 %copy.100 = bf16[4,80,2,1280]{3,2,1,0:T(2,128)(2,1)} copy(bf16[4,80,2,1280]{3,0,2,1:T(4,128)(2,1)S(1)} %fusion.21) | data formatting | bytes 3276800 | tf_op jit(solution)/shard_map/convert_element_type | solution.py:107
  (87 shorter events, 23.6 us)
Async XLA Ops:
  0.9 0.6 copy-start.2
  5.1 6.5 %copy-start.10 = (f32[32]{0:T(128)S(1)}, f32[32]{0:T(128)}, u32[]{:S(2)}) copy-start(f32[32]{0:T(128)} %param.11) | copy-start | bytes 388
  5.1 14.3 %copy-start.7 = (s32[1280]{0:T(1024)S(1)}, s32[1280]{0:T(1024)}, u32[]{:S(2)}) copy-start(s32[1280]{0:T(1024)} %param.9) | copy-start | bytes 15364
  12.6 15.9 %all-to-all-start = ((bf16[4,80,2,64]{1,2,0,3:T(2,128)(2,1)}), bf16[4,80,2,64]{1,2,0,3:T(2,128)(2,1)S(1)}, u32[]{:S(2)}, u32[]{:S(2)}) async-start(bf16[4,80,2,64]{1,2,0,3:T(2,128)(2,1)} %copy.81), calls=%async_computation | async-start | bytes 262144 | tf_op jit(solution)/shard_map/all_to_all | solution.py:62
  21.2 2.5 %copy-start.8 = (s32[4,4,4]{2,1,0:T(4,128)S(1)}, s32[4,4,4]{2,1,0:T(4,128)}, u32[]{:S(2)}) copy-start(s32[4,4,4]{2,1,0:T(4,128)} %param.13) | copy-start | bytes 772
  30.2 8.2 %collective-permute-start = (bf16[1280,2,4]{0,2,1:T(4,128)(2,1)S(1)}, bf16[1280,2,4]{0,2,1:T(4,128)(2,1)S(1)}, u32[]{:S(2)}, u32[]{:S(2)}) collective-permute-start(bf16[1280,2,4]{0,2,1:T(4,128)(2,1)S(1)} %convert_element_type.122), channel_id=1, source_target_pairs={{0,1},{1,2},{2,3},{3,4},{4,5},{5,6},{6,7},{7,8},{8,9},{9,10},{10,1... | collective-permute-start | bytes 61448 | tf_op jit(solution)/shard_map/ppermute | solution.py:36
  38.3 4.5 %collective-permute-start.1 = (bf16[1280,2,4]{0,2,1:T(4,128)(2,1)S(1)}, bf16[1280,2,4]{0,2,1:T(4,128)(2,1)S(1)}, u32[]{:S(2)}, u32[]{:S(2)}) collective-permute-start(bf16[1280,2,4]{0,2,1:T(4,128)(2,1)S(1)} %fusion.79), channel_id=1, source_target_pairs={{0,2},{1,3},{2,4},{3,5},{4,6},{5,7},{6,8},{7,9},{8,10},{9,11},{10,... | collective-permute-start | bytes 61448 | tf_op jit(solution)/shard_map/ppermute | solution.py:36
  42.9 5.4 %collective-permute-start.2 = (bf16[1280,2,4]{0,2,1:T(4,128)(2,1)S(1)}, bf16[1280,2,4]{0,2,1:T(4,128)(2,1)S(1)}, u32[]{:S(2)}, u32[]{:S(2)}) collective-permute-start(bf16[1280,2,4]{0,2,1:T(4,128)(2,1)S(1)} %fusion.106), channel_id=1, source_target_pairs={{0,4},{1,5},{2,6},{3,7},{4,8},{5,9},{6,10},{7,11},{8,12},{9,13},{1... | collective-permute-start | bytes 61448 | tf_op jit(solution)/shard_map/ppermute | solution.py:36
  46.2 20.4 %copy-start = (bf16[1284,1280]{1,0:T(8,128)(2,1)S(1)}, bf16[1284,1280]{1,0:T(8,128)(2,1)}, u32[]{:S(2)}) copy-start(bf16[1284,1280]{1,0:T(8,128)(2,1)} %slice.48) | copy-start | bytes 9861124
  48.4 4.5 %collective-permute-start.3 = (bf16[1280,2,4]{0,2,1:T(4,128)(2,1)S(1)}, bf16[1280,2,4]{0,2,1:T(4,128)(2,1)S(1)}, u32[]{:S(2)}, u32[]{:S(2)}) collective-permute-start(bf16[1280,2,4]{0,2,1:T(4,128)(2,1)S(1)} %fusion.80), channel_id=1, source_target_pairs={{0,8},{1,9},{2,10},{3,11},{4,12},{5,13},{6,14},{7,15},{16,24},{17,... | collective-permute-start | bytes 61448 | tf_op jit(solution)/shard_map/ppermute | solution.py:36
  52.9 17.9 %collective-permute-start.4 = (bf16[1280,2,4]{0,2,1:T(4,128)(2,1)S(1)}, bf16[1280,2,4]{0,2,1:T(4,128)(2,1)S(1)}, u32[]{:S(2)}, u32[]{:S(2)}) collective-permute-start(bf16[1280,2,4]{0,2,1:T(4,128)(2,1)S(1)} %add_convert_fusion.3), channel_id=1, source_target_pairs={{0,1},{1,2},{2,3},{3,4},{4,5},{5,6},{6,7},{7,8},{8,9},{9,10},{10,1... | collective-permute-start | bytes 61448 | tf_op jit(solution)/shard_map/ppermute | solution.py:41
  70.8 1.9 %copy-start.1 = (bf16[1284,1280]{1,0:T(8,128)(2,1)S(1)}, bf16[1284,1280]{1,0:T(8,128)(2,1)}, u32[]{:S(2)}) copy-start(bf16[1284,1280]{1,0:T(8,128)(2,1)} %slice.48) | copy-start | bytes 9861124
  70.8 3.0 %copy-start.4 = (f32[4,4,4,1284]{3,2,1,0:T(4,128)S(1)}, f32[4,4,4,1284]{3,2,1,0:T(4,128)}, u32[]{:S(2)}) copy-start(f32[4,4,4,1284]{3,2,1,0:T(4,128)} %reshape.200) | copy-start | bytes 986116
  70.9 3.0 %copy-start.5 = (f32[4,4,4,1284]{3,0,1,2:T(4,128)S(1)}, f32[4,4,4,1284]{3,0,1,2:T(4,128)}, u32[]{:S(2)}) copy-start(f32[4,4,4,1284]{3,0,1,2:T(4,128)} %fusion.28) | copy-start | bytes 986116
  70.9 3.0 %copy-start.6 = (f32[4,4,4,1284]{3,0,1,2:T(4,128)S(1)}, f32[4,4,4,1284]{3,0,1,2:T(4,128)}, u32[]{:S(2)}) copy-start(f32[4,4,4,1284]{3,0,1,2:T(4,128)} %reduce_window_sum.11) | copy-start | bytes 986116
  70.9 3.0 %copy-start.9 = (f32[4,4,4]{0,2,1:T(4,128)S(1)}, f32[4,4,4]{0,2,1:T(4,128)}, u32[]{:S(2)}) copy-start(f32[4,4,4]{0,2,1:T(4,128)} %copy.76) | copy-start | bytes 772
  70.9 3.0 %copy-start.11 = (f32[4]{0:T(128)S(1)}, f32[4]{0:T(128)}, u32[]{:S(2)}) copy-start(f32[4]{0:T(128)} %param.15) | copy-start | bytes 52
  70.9 3.0 %copy-start.12 = (s32[1,4]{1,0:T(1,128)S(1)}, s32[1,4]{1,0:T(1,128)}, u32[]{:S(2)}) copy-start(s32[1,4]{1,0:T(1,128)} %param.14) | copy-start | bytes 52
  87.3 13.8 %all-to-all-start.1 = ((bf16[16,4,2,2,2,80]{5,1,4,2,3,0:T(4,128)(2,1)}), bf16[16,4,2,2,2,80]{5,1,4,2,3,0:T(4,128)(2,1)S(1)}, u32[]{:S(2)}, u32[]{:S(2)}) async-start(bf16[16,4,2,2,2,80]{5,1,4,2,3,0:T(4,128)(2,1)} %constant_dynamic-update-slice_fusion), calls=%async_computation.1 | async-start | bytes 262144 | tf_op jit(solution)/shard_map/all_to_all | solution.py:102
  101.4 4.2 %copy-start.3 = (pred[80,1280]{1,0:T(8,128)(4,1)S(1)}, pred[80,1280]{1,0:T(8,128)(4,1)}, u32[]{:S(2)}) copy-start(pred[80,1280]{1,0:T(8,128)(4,1)} %copy-done.2) | copy-start | bytes 307204
